TPU v7x, 32 devices: a whole 2x2x4 slice. The times are simulated.
32 devices in a mesh: gx: 4 (over y, x), gy: 8 (over z, core).
Axes of the slice: x: 2, y: 2, z: 4, core: 2. Of those that a mesh axis runs over, the one named last changes fastest.
Arguments:
- height: float32 [1, 2048, 4096], P(None, 'gy', 'gx'), may hold values from -12 to 12
- zonal_velocity: float32 [1, 2048, 4096], P(None, 'gy', 'gx'), may hold values from -4 to 4
- meridional_velocity: float32 [1, 2048, 4096], P(None, 'gy', 'gx'), may hold values from -4 to 4
- wave_courant: float32 [1], replicated, may hold values from 4 to 24
Outputs:
- solution: float32 [1, 2048, 4096], P(None, 'gy', 'gx')
- new_zonal: float32 [1, 2048, 4096], P(None, 'gy', 'gx')
- new_meridional: float32 [1, 2048, 4096], P(None, 'gy', 'gx')
All inputs are finite; a program needn't handle non-finite values.
Results may differ from a plain program's by a relative error of at most 0.0003.
Values sent between devices are 32-bit elements; how exact they have to be, the bound alone decides.
A program may use at most 64 MiB of HBM per device.

v0:
```python
import jax
import jax.numpy as jnp
from jax import lax
from jax.sharding import PartitionSpec as P

ITERS = 3


advect_courant = 0.2
implicit_weight = 0.25
explicit_weight = 0.5


def extended(block, sides, width):
    for axis, dim in sides:
        count = lax.axis_size(axis)
        forward = [(i, i + 1) for i in range(count - 1)]
        forward.append((count - 1, 0))
        backward = [(target, source) for source, target in forward]
        low = lax.ppermute(
            lax.slice_in_dim(block, block.shape[dim] - width, None, axis=dim), axis, forward
        )
        high = lax.ppermute(lax.slice_in_dim(block, 0, width, axis=dim), axis, backward)
        block = jnp.concatenate([low, block, high], axis=dim)
    return block


def inner_cells(padded):
    return padded[:, 1:-1, 1:-1]


def centered_zonal(padded):
    return 0.5 * (padded[:, 1:-1, 2:] - padded[:, 1:-1, :-2])


def centered_meridional(padded):
    return 0.5 * (padded[:, 2:, 1:-1] - padded[:, :-2, 1:-1])


def upwind_zonal(padded, speed):
    middle = padded[:, 1:-1, 1:-1]
    backward = middle - padded[:, 1:-1, :-2]
    forward = padded[:, 1:-1, 2:] - middle
    return speed * jnp.where(speed > 0, backward, forward)


def upwind_meridional(padded, speed):
    middle = padded[:, 1:-1, 1:-1]
    backward = middle - padded[:, :-2, 1:-1]
    forward = padded[:, 2:, 1:-1] - middle
    return speed * jnp.where(speed > 0, backward, forward)


def advection(padded, zonal_pad, meridional_pad):
    zonal_speed = inner_cells(zonal_pad)
    meridional_speed = inner_cells(meridional_pad)
    return -(upwind_zonal(padded, zonal_speed) + upwind_meridional(padded, meridional_speed))


def section_values(stacked_pad, wave_factor):
    height_pad = stacked_pad[0]
    zonal_pad = stacked_pad[1]
    meridional_pad = stacked_pad[2]
    factor = explicit_weight * advect_courant
    section_height = (
        inner_cells(height_pad)
        + factor * advection(height_pad, zonal_pad, meridional_pad)
        - wave_factor * (centered_zonal(zonal_pad) + centered_meridional(meridional_pad))
    )
    section_zonal = (
        inner_cells(zonal_pad)
        + factor * advection(zonal_pad, zonal_pad, meridional_pad)
        - wave_factor * centered_zonal(height_pad)
    )
    section_meridional = (
        inner_cells(meridional_pad)
        + factor * advection(meridional_pad, zonal_pad, meridional_pad)
        - wave_factor * centered_meridional(height_pad)
    )
    return (section_height, section_zonal, section_meridional)


def helmholtz_padded(padded, stiffness):
    middle = padded[:, 2:-2, 2:-2]
    second = (
        padded[:, 2:-2, 4:]
        + padded[:, 2:-2, :-4]
        + padded[:, 4:, 2:-2]
        + padded[:, :-4, 2:-2]
        - 4.0 * middle
    ) * 0.25
    return middle - stiffness * second


def sweep_operator(values, stiffness):
    padded = extended(values, (("gy", 1), ("gx", 2)), 2)
    return helmholtz_padded(padded, stiffness)


def direction_operator(values, stiffness):
    padded = extended(values, (("gy", 1), ("gx", 2)), 2)
    return helmholtz_padded(padded, stiffness)


def chebyshev(residual, stiffness):
    upper = 1.0 + 2.0 * stiffness
    center = (upper + 1.0) * 0.5
    half_width = (upper - 1.0) * 0.5
    ratio = center / half_width
    rho_prev = 1.0 / ratio
    update = residual / center
    approx = update
    for sweep_index in range(3):
        misfit = residual - sweep_operator(approx, stiffness)
        rho_next = 1.0 / (2.0 * ratio - rho_prev)
        update = rho_next * rho_prev * update + 2.0 * rho_next / half_width * misfit
        approx = approx + update
        rho_prev = rho_next
    return approx


def local_sum(values):
    return jnp.sum(values, axis=(1, 2))


def joint_products(residual, precond, product):
    first_total, second_total = lax.psum(
        (local_sum(residual * precond), local_sum(precond * product)), ("gx", "gy")
    )
    return (first_total.reshape(-1, 1, 1), second_total.reshape(-1, 1, 1))


def local(height, zonal_velocity, meridional_velocity, wave_courant):
    wave_factor = (implicit_weight * wave_courant).reshape(-1, 1, 1)
    stacked = jnp.stack((height, zonal_velocity, meridional_velocity))
    stacked_pad = extended(stacked, (("gy", 2), ("gx", 3)), 1)
    section_height, section_zonal, section_meridional = section_values(stacked_pad, wave_factor)
    velocity_pad = extended(
        jnp.stack((section_zonal, section_meridional)), (("gy", 2), ("gx", 3)), 1
    )
    source = section_height - wave_factor * (
        centered_zonal(velocity_pad[0]) + centered_meridional(velocity_pad[1])
    )
    stiffness = wave_factor * wave_factor
    solution = jnp.zeros_like(source)
    residual = source
    precond = chebyshev(residual, stiffness)
    product = direction_operator(precond, stiffness)
    precond_norm, curvature = joint_products(residual, precond, product)
    step_length = precond_norm / curvature
    direction = precond
    along = product
    for iteration in range(ITERS):
        solution = solution + step_length * direction
        residual = residual - step_length * along
        if iteration + 1 < ITERS:
            precond = chebyshev(residual, stiffness)
            product = direction_operator(precond, stiffness)
            norm_next, curvature = joint_products(residual, precond, product)
            beta_ratio = norm_next / precond_norm
            step_length = norm_next / (curvature - beta_ratio * norm_next / step_length)
            direction = precond + beta_ratio * direction
            along = product + beta_ratio * along
            precond_norm = norm_next
    solved_pad = extended(solution, (("gy", 1), ("gx", 2)), 1)
    new_zonal = section_zonal - wave_factor * centered_zonal(solved_pad)
    new_meridional = section_meridional - wave_factor * centered_meridional(solved_pad)
    return (solution, new_zonal, new_meridional)


def solution(mesh):
    return jax.shard_map(
        local,
        mesh=mesh,
        in_specs=(P(None, "gy", "gx"), P(None, "gy", "gx"), P(None, "gy", "gx"), P()),
        out_specs=(P(None, "gy", "gx"), P(None, "gy", "gx"), P(None, "gy", "gx")),
        check_vma=False,
    )
```

profile of v0, /device:TPU:0, one launch (start us, length us, event | category | flops | bytes accessed | tf_op | source)
XLA Modules:
  0.0 398.0 jit_solution(3621294102384342756)
XLA Ops:
  2.2 4.1 %collective-permute-start.1 = (f32[3,1,1,1024]{3,2,1,0:T(1,128)S(1)}, f32[3,1,1,1024]{3,2,1,0:T(1,128)S(1)}, u32[]{:S(2)}, u32[]{:S(2)}) collective-permute-start(f32[3,1,1,1024]{3,2,1,0:T(1,128)S(1)} %get-tuple-element.36), channel_id=1, source_target_pairs={{1,0},{2,1},{3,2},{4,3},{5,4},{6,5},{7,6},{0,7},{9,8},{10,9},{11,1... | collective-permute-start | bytes 36872 | tf_op jit(solution)/shard_map/ppermute | solution.py:23
  12.0 9.7 %collective-permute-done.2 = f32[3,1,258,1]{3,2,1,0:T(8,128)} collective-permute-done((f32[3,1,258,1]{3,2,1,0:T(8,128)S(1)}, f32[3,1,258,1]{3,2,1,0:T(8,128)}, u32[]{:S(2)}, u32[]{:S(2)}) %collective-permute-start.2) | collective-permute-done | bytes 3128 | tf_op jit(solution)/shard_map/ppermute | solution.py:20
  21.6 8.3 %collective-permute-done.3 = f32[3,1,258,1]{3,2,1,0:T(8,128)} collective-permute-done((f32[3,1,258,1]{3,2,1,0:T(8,128)S(1)}, f32[3,1,258,1]{3,2,1,0:T(8,128)}, u32[]{:S(2)}, u32[]{:S(2)}) %collective-permute-start.3) | collective-permute-done | bytes 3128 | tf_op jit(solution)/shard_map/ppermute | solution.py:23
  29.9 4.4 %concatenate.221 = f32[3,1,258,1026]{3,2,1,0:T(8,128)} concatenate(f32[3,1,258,1]{3,2,1,0:T(8,128)} %collective-permute-done.2, f32[3,1,258,1024]{3,2,1,0:T(8,128)S(1)} %pad_maximum_fusion, f32[3,1,258,1]{3,2,1,0:T(8,128)} %collective-permute-done.3), dimensions={3} | concatenate | bytes 6352992 | tf_op jit(solution)/shard_map/concatenate | solution.py:24
  40.8 3.5 collective-permute-start.5
  51.7 7.3 %collective-permute-done.6 = f32[2,1,258,1]{3,2,1,0:T(8,128)S(1)} collective-permute-done((f32[2,1,258,1]{3,2,1,0:T(8,128)S(1)}, f32[2,1,258,1]{3,2,1,0:T(8,128)S(1)}, u32[]{:S(2)}, u32[]{:S(2)}) %collective-permute-start.6) | collective-permute-done | bytes 2096 | tf_op jit(solution)/shard_map/ppermute | solution.py:20
  61.1 4.2 %concatenate.223 = f32[2,1,258,1026]{3,2,1,0:T(8,128)} concatenate(f32[2,1,258,1]{3,2,1,0:T(8,128)S(1)} %collective-permute-done.6, f32[2,1,258,1024]{3,2,1,0:T(8,128)} %pad_maximum_fusion.1, f32[2,1,258,1]{3,2,1,0:T(8,128)S(1)} %collective-permute-done.7), dimensions={3} | concatenate | bytes 4235328 | tf_op jit(solution)/shard_map/concatenate | solution.py:24
  67.5 3.8 broadcast_divide_fusion.2
  71.3 3.5 collective-permute-start.9
  76.3 2.5 collective-permute-start.10
  79.0 3.5 collective-permute-done.10
  85.8 3.5 collective-permute-start.13
  93.0 2.9 collective-permute-done.14
  97.6 3.4 fusion.132
  101.1 3.5 collective-permute-start.17
  108.3 2.9 collective-permute-done.18
  114.6 3.5 collective-permute-start.21
  121.7 3.0 collective-permute-done.22
  127.8 39.1 %all-reduce.2 = (f32[1,1,1]{2,1,0:T(1,128)}, f32[1,1,1]{2,1,0:T(1,128)}) all-reduce(f32[1,1,1]{2,1,0:T(1,128)} %bitcast.20, f32[1,1,1]{2,1,0:T(1,128)} %bitcast.21), channel_id=1, replica_groups=mesh['gx'=4,'gy'=8] {'gx','gy'}, use_global_device_ids=true, to_apply=%region_1.2 | all-reduce | flops 2 | bytes 16 | tf_op jit(solution)/shard_map/psum | solution.py:127
  169.2 3.5 collective-permute-start.25
  174.2 3.2 collective-permute-start.26
  177.5 4.0 collective-permute-done.26
  181.5 2.7 collective-permute-done.27
  185.1 3.5 collective-permute-start.29
  192.2 4.1 %collective-permute-done.30 = f32[1,260,2]{2,1,0:T(8,128)S(1)} collective-permute-done((f32[1,260,2]{2,1,0:T(8,128)S(1)}, f32[1,260,2]{2,1,0:T(8,128)S(1)}, u32[]{:S(2)}, u32[]{:S(2)}) %collective-permute-start.30) | collective-permute-done | bytes 2112 | tf_op jit(solution)/shard_map/ppermute | solution.py:23
  197.3 3.4 fusion.130
  200.8 3.5 collective-permute-start.33
  208.0 3.6 collective-permute-done.34
  214.9 3.5 collective-permute-start.37
  222.0 3.8 collective-permute-done.38
  227.8 2.5 multiply_reduce_fusion.1
  230.3 38.5 %all-reduce.1 = (f32[1,1,1]{2,1,0:T(1,128)}, f32[1,1,1]{2,1,0:T(1,128)}) all-reduce(f32[1,1,1]{2,1,0:T(1,128)} %bitcast.23, f32[1,1,1]{2,1,0:T(1,128)} %bitcast.24), channel_id=1, replica_groups=mesh['gx'=4,'gy'=8] {'gx','gy'}, use_global_device_ids=true, to_apply=%region_5.6 | all-reduce | flops 2 | bytes 16 | tf_op jit(solution)/shard_map/psum | solution.py:127
  273.3 4.3 %broadcast_divide_fusion = (f32[1,256,1024]{2,1,0:T(8,128)S(1)}, f32[1,256,1024]{2,1,0:T(8,128)S(1)}) fusion(f32[]{:T(128)} %bitcast.12, f32[1,256,1024]{2,1,0:T(8,128)S(1)} %get-tuple-element.22, f32[1,256,1024]{2,1,0:T(8,128)S(1)} %fusion.87, f32[1,2,1024]{2,1,0:T(2,128)} %copy-done.18, f32[1,2,1024]{2,1,0:T(2,128)} %copy-done.19, ...), kind=kLoop, calls=%fused_computation.253 | loop fusion | flops 9175040 | bytes 5283984 | tf_op jit(solution)/shard_map/div | solution.py:111
  277.7 3.5 collective-permute-start.41
  285.2 4.2 %collective-permute-done.42 = f32[1,260,2]{2,1,0:T(8,128)S(1)} collective-permute-done((f32[1,260,2]{2,1,0:T(8,128)S(1)}, f32[1,260,2]{2,1,0:T(8,128)S(1)}, u32[]{:S(2)}, u32[]{:S(2)}) %collective-permute-start.42) | collective-permute-done | bytes 2112 | tf_op jit(solution)/shard_map/ppermute | solution.py:23
  289.3 3.8 collective-permute-done.43
  294.1 3.5 collective-permute-start.45
  301.2 4.0 collective-permute-done.46
  306.5 3.4 fusion.128
  310.0 3.5 collective-permute-start.49
  317.1 4.2 %collective-permute-done.50 = f32[1,260,2]{2,1,0:T(8,128)S(1)} collective-permute-done((f32[1,260,2]{2,1,0:T(8,128)S(1)}, f32[1,260,2]{2,1,0:T(8,128)S(1)}, u32[]{:S(2)}, u32[]{:S(2)}) %collective-permute-start.50) | collective-permute-done | bytes 2112 | tf_op jit(solution)/shard_map/ppermute | solution.py:23
  324.0 3.5 collective-permute-start.53
  331.1 3.2 collective-permute-done.54
  337.9 38.2 %all-reduce = (f32[1,1,1]{2,1,0:T(1,128)}, f32[1,1,1]{2,1,0:T(1,128)}) all-reduce(f32[1,1,1]{2,1,0:T(1,128)} %bitcast.27, f32[1,1,1]{2,1,0:T(1,128)} %bitcast.28), channel_id=1, replica_groups=mesh['gx'=4,'gy'=8] {'gx','gy'}, use_global_device_ids=true, to_apply=%region_9.10 | all-reduce | flops 2 | bytes 16 | tf_op jit(solution)/shard_map/psum | solution.py:127
  380.5 3.5 collective-permute-start.57
  385.4 3.3 collective-permute-start.58
  388.8 4.0 collective-permute-done.58
  392.7 3.2 collective-permute-done.59
  (174 shorter events, 96.3 us)
Async XLA Ops:
  1.7 6.0 %collective-permute-start = (f32[3,1,1,1024]{3,2,1,0:T(1,128)S(1)}, f32[3,1,1,1024]{3,2,1,0:T(1,128)S(1)}, u32[]{:S(2)}, u32[]{:S(2)}) collective-permute-start(f32[3,1,1,1024]{3,2,1,0:T(1,128)S(1)} %get-tuple-element.35), channel_id=1, source_target_pairs={{0,1},{1,2},{2,3},{3,4},{4,5},{5,6},{6,7},{7,0},{8,9},{9,10},{10,1... | collective-permute-start | bytes 36872 | tf_op jit(solution)/shard_map/ppermute | solution.py:20
  2.2 5.5 %collective-permute-start.1 = (f32[3,1,1,1024]{3,2,1,0:T(1,128)S(1)}, f32[3,1,1,1024]{3,2,1,0:T(1,128)S(1)}, u32[]{:S(2)}, u32[]{:S(2)}) collective-permute-start(f32[3,1,1,1024]{3,2,1,0:T(1,128)S(1)} %get-tuple-element.36), channel_id=1, source_target_pairs={{1,0},{2,1},{3,2},{4,3},{5,4},{6,5},{7,6},{0,7},{9,8},{10,9},{11,1... | collective-permute-start | bytes 36872 | tf_op jit(solution)/shard_map/ppermute | solution.py:23
  8.3 13.3 %collective-permute-start.2 = (f32[3,1,258,1]{3,2,1,0:T(8,128)S(1)}, f32[3,1,258,1]{3,2,1,0:T(8,128)}, u32[]{:S(2)}, u32[]{:S(2)}) collective-permute-start(f32[3,1,258,1]{3,2,1,0:T(8,128)S(1)} %get-tuple-element.34), channel_id=1, source_target_pairs={{0,8},{8,16},{16,24},{24,0},{1,9},{9,17},{17,25},{25,1},{2,10},{10... | collective-permute-start | bytes 9296 | tf_op jit(solution)/shard_map/ppermute | solution.py:20
  10.3 19.6 %collective-permute-start.3 = (f32[3,1,258,1]{3,2,1,0:T(8,128)S(1)}, f32[3,1,258,1]{3,2,1,0:T(8,128)}, u32[]{:S(2)}, u32[]{:S(2)}) collective-permute-start(f32[3,1,258,1]{3,2,1,0:T(8,128)S(1)} %get-tuple-element.33), channel_id=1, source_target_pairs={{8,0},{16,8},{24,16},{0,24},{9,1},{17,9},{25,17},{1,25},{10,2},{18... | collective-permute-start | bytes 9296 | tf_op jit(solution)/shard_map/ppermute | solution.py:23
  40.8 5.0 %collective-permute-start.4 = (f32[2,1,1,1024]{3,2,1,0:T(1,128)S(1)}, f32[2,1,1,1024]{3,2,1,0:T(1,128)S(1)}, u32[]{:S(2)}, u32[]{:S(2)}) collective-permute-start(f32[2,1,1,1024]{3,2,1,0:T(1,128)S(1)} %get-tuple-element.41), channel_id=1, source_target_pairs={{0,1},{1,2},{2,3},{3,4},{4,5},{5,6},{6,7},{7,0},{8,9},{9,10},{10,1... | collective-permute-start | bytes 24584 | tf_op jit(solution)/shard_map/ppermute | solution.py:20
  48.7 10.3 %collective-permute-start.6 = (f32[2,1,258,1]{3,2,1,0:T(8,128)S(1)}, f32[2,1,258,1]{3,2,1,0:T(8,128)S(1)}, u32[]{:S(2)}, u32[]{:S(2)}) collective-permute-start(f32[2,1,258,1]{3,2,1,0:T(8,128)S(1)} %get-tuple-element.40), channel_id=1, source_target_pairs={{0,8},{8,16},{16,24},{24,0},{1,9},{9,17},{17,25},{25,1},{2,10},{10... | collective-permute-start | bytes 6200 | tf_op jit(solution)/shard_map/ppermute | solution.py:20
  50.2 10.9 %collective-permute-start.7 = (f32[2,1,258,1]{3,2,1,0:T(8,128)S(1)}, f32[2,1,258,1]{3,2,1,0:T(8,128)S(1)}, u32[]{:S(2)}, u32[]{:S(2)}) collective-permute-start(f32[2,1,258,1]{3,2,1,0:T(8,128)S(1)} %get-tuple-element.39), channel_id=1, source_target_pairs={{8,0},{16,8},{24,16},{0,24},{9,1},{17,9},{25,17},{1,25},{10,2},{18... | collective-permute-start | bytes 6200 | tf_op jit(solution)/shard_map/ppermute | solution.py:23
  71.2 5.0 %collective-permute-start.8 = (f32[1,2,1024]{2,1,0:T(2,128)S(1)}, f32[1,2,1024]{2,1,0:T(2,128)S(1)}, u32[]{:S(2)}, u32[]{:S(2)}) collective-permute-start(f32[1,2,1024]{2,1,0:T(2,128)S(1)} %get-tuple-element.96), channel_id=1, source_target_pairs={{0,1},{1,2},{2,3},{3,4},{4,5},{5,6},{6,7},{7,0},{8,9},{9,10},{10,1... | collective-permute-start | bytes 24584 | tf_op jit(solution)/shard_map/ppermute | solution.py:20
  71.3 4.9 %collective-permute-start.9 = (f32[1,2,1024]{2,1,0:T(2,128)S(1)}, f32[1,2,1024]{2,1,0:T(2,128)S(1)}, u32[]{:S(2)}, u32[]{:S(2)}) collective-permute-start(f32[1,2,1024]{2,1,0:T(2,128)S(1)} %get-tuple-element.95), channel_id=1, source_target_pairs={{1,0},{2,1},{3,2},{4,3},{5,4},{6,5},{7,6},{0,7},{9,8},{10,9},{11,1... | collective-permute-start | bytes 24584 | tf_op jit(solution)/shard_map/ppermute | solution.py:23
  76.3 6.1 %collective-permute-start.10 = (f32[1,260,2]{2,1,0:T(8,128)S(1)}, f32[1,260,2]{2,1,0:T(8,128)S(1)}, u32[]{:S(2)}, u32[]{:S(2)}) collective-permute-start(f32[1,260,2]{2,1,0:T(8,128)S(1)} %get-tuple-element.65), channel_id=1, source_target_pairs={{8,0},{16,8},{24,16},{0,24},{9,1},{17,9},{25,17},{1,25},{10,2},{18... | collective-permute-start | bytes 6248 | tf_op jit(solution)/shard_map/ppermute | solution.py:23
  78.8 6.0 %collective-permute-start.11 = (f32[1,260,2]{2,1,0:T(8,128)S(1)}, f32[1,260,2]{2,1,0:T(8,128)S(1)}, u32[]{:S(2)}, u32[]{:S(2)}) collective-permute-start(f32[1,260,2]{2,1,0:T(8,128)S(1)} %get-tuple-element.66), channel_id=1, source_target_pairs={{0,8},{8,16},{16,24},{24,0},{1,9},{9,17},{17,25},{25,1},{2,10},{10... | collective-permute-start | bytes 6248 | tf_op jit(solution)/shard_map/ppermute | solution.py:20
  85.8 4.9 %collective-permute-start.12 = (f32[1,2,1024]{2,1,0:T(2,128)S(1)}, f32[1,2,1024]{2,1,0:T(2,128)S(1)}, u32[]{:S(2)}, u32[]{:S(2)}) collective-permute-start(f32[1,2,1024]{2,1,0:T(2,128)S(1)} %get-tuple-element.94), channel_id=1, source_target_pairs={{0,1},{1,2},{2,3},{3,4},{4,5},{5,6},{6,7},{7,0},{8,9},{9,10},{10,1... | collective-permute-start | bytes 24584 | tf_op jit(solution)/shard_map/ppermute | solution.py:20
  90.9 5.1 %collective-permute-start.14 = (f32[1,260,2]{2,1,0:T(8,128)S(1)}, f32[1,260,2]{2,1,0:T(8,128)S(1)}, u32[]{:S(2)}, u32[]{:S(2)}) collective-permute-start(f32[1,260,2]{2,1,0:T(8,128)S(1)} %get-tuple-element.63), channel_id=1, source_target_pairs={{8,0},{16,8},{24,16},{0,24},{9,1},{17,9},{25,17},{1,25},{10,2},{18... | collective-permute-start | bytes 6248 | tf_op jit(solution)/shard_map/ppermute | solution.py:23
  91.7 5.9 %collective-permute-start.15 = (f32[1,260,2]{2,1,0:T(8,128)S(1)}, f32[1,260,2]{2,1,0:T(8,128)S(1)}, u32[]{:S(2)}, u32[]{:S(2)}) collective-permute-start(f32[1,260,2]{2,1,0:T(8,128)S(1)} %get-tuple-element.64), channel_id=1, source_target_pairs={{0,8},{8,16},{16,24},{24,0},{1,9},{9,17},{17,25},{25,1},{2,10},{10... | collective-permute-start | bytes 6248 | tf_op jit(solution)/shard_map/ppermute | solution.py:20
  101.1 4.9 %collective-permute-start.16 = (f32[1,2,1024]{2,1,0:T(2,128)S(1)}, f32[1,2,1024]{2,1,0:T(2,128)S(1)}, u32[]{:S(2)}, u32[]{:S(2)}) collective-permute-start(f32[1,2,1024]{2,1,0:T(2,128)S(1)} %get-tuple-element.92), channel_id=1, source_target_pairs={{0,1},{1,2},{2,3},{3,4},{4,5},{5,6},{6,7},{7,0},{8,9},{9,10},{10,1... | collective-permute-start | bytes 24584 | tf_op jit(solution)/shard_map/ppermute | solution.py:20
  106.2 5.1 %collective-permute-start.18 = (f32[1,260,2]{2,1,0:T(8,128)S(1)}, f32[1,260,2]{2,1,0:T(8,128)S(1)}, u32[]{:S(2)}, u32[]{:S(2)}) collective-permute-start(f32[1,260,2]{2,1,0:T(8,128)S(1)} %get-tuple-element.61), channel_id=1, source_target_pairs={{8,0},{16,8},{24,16},{0,24},{9,1},{17,9},{25,17},{1,25},{10,2},{18... | collective-permute-start | bytes 6248 | tf_op jit(solution)/shard_map/ppermute | solution.py:23
  107.7 5.9 %collective-permute-start.19 = (f32[1,260,2]{2,1,0:T(8,128)S(1)}, f32[1,260,2]{2,1,0:T(8,128)S(1)}, u32[]{:S(2)}, u32[]{:S(2)}) collective-permute-start(f32[1,260,2]{2,1,0:T(8,128)S(1)} %get-tuple-element.62), channel_id=1, source_target_pairs={{0,8},{8,16},{16,24},{24,0},{1,9},{9,17},{17,25},{25,1},{2,10},{10... | collective-permute-start | bytes 6248 | tf_op jit(solution)/shard_map/ppermute | solution.py:20
  114.5 5.0 %collective-permute-start.20 = (f32[1,2,1024]{2,1,0:T(2,128)S(1)}, f32[1,2,1024]{2,1,0:T(2,128)S(1)}, u32[]{:S(2)}, u32[]{:S(2)}) collective-permute-start(f32[1,2,1024]{2,1,0:T(2,128)S(1)} %get-tuple-element.90), channel_id=1, source_target_pairs={{0,1},{1,2},{2,3},{3,4},{4,5},{5,6},{6,7},{7,0},{8,9},{9,10},{10,1... | collective-permute-start | bytes 24584 | tf_op jit(solution)/shard_map/ppermute | solution.py:20
  114.6 4.9 %collective-permute-start.21 = (f32[1,2,1024]{2,1,0:T(2,128)S(1)}, f32[1,2,1024]{2,1,0:T(2,128)S(1)}, u32[]{:S(2)}, u32[]{:S(2)}) collective-permute-start(f32[1,2,1024]{2,1,0:T(2,128)S(1)} %get-tuple-element.89), channel_id=1, source_target_pairs={{1,0},{2,1},{3,2},{4,3},{5,4},{6,5},{7,6},{0,7},{9,8},{10,9},{11,1... | collective-permute-start | bytes 24584 | tf_op jit(solution)/shard_map/ppermute | solution.py:23
  119.6 5.1 %collective-permute-start.22 = (f32[1,260,2]{2,1,0:T(8,128)S(1)}, f32[1,260,2]{2,1,0:T(8,128)S(1)}, u32[]{:S(2)}, u32[]{:S(2)}) collective-permute-start(f32[1,260,2]{2,1,0:T(8,128)S(1)} %get-tuple-element.59), channel_id=1, source_target_pairs={{8,0},{16,8},{24,16},{0,24},{9,1},{17,9},{25,17},{1,25},{10,2},{18... | collective-permute-start | bytes 6248 | tf_op jit(solution)/shard_map/ppermute | solution.py:23
  120.3 5.9 %collective-permute-start.23 = (f32[1,260,2]{2,1,0:T(8,128)S(1)}, f32[1,260,2]{2,1,0:T(8,128)S(1)}, u32[]{:S(2)}, u32[]{:S(2)}) collective-permute-start(f32[1,260,2]{2,1,0:T(8,128)S(1)} %get-tuple-element.60), channel_id=1, source_target_pairs={{0,8},{8,16},{16,24},{24,0},{1,9},{9,17},{17,25},{25,1},{2,10},{10... | collective-permute-start | bytes 6248 | tf_op jit(solution)/shard_map/ppermute | solution.py:20
  169.2 4.9 %collective-permute-start.24 = (f32[1,2,1024]{2,1,0:T(2,128)S(1)}, f32[1,2,1024]{2,1,0:T(2,128)S(1)}, u32[]{:S(2)}, u32[]{:S(2)}) collective-permute-start(f32[1,2,1024]{2,1,0:T(2,128)S(1)} %get-tuple-element.88), channel_id=1, source_target_pairs={{0,1},{1,2},{2,3},{3,4},{4,5},{5,6},{6,7},{7,0},{8,9},{9,10},{10,1... | collective-permute-start | bytes 24584 | tf_op jit(solution)/shard_map/ppermute | solution.py:20
  174.2 7.2 %collective-permute-start.26 = (f32[1,260,2]{2,1,0:T(8,128)S(1)}, f32[1,260,2]{2,1,0:T(8,128)S(1)}, u32[]{:S(2)}, u32[]{:S(2)}) collective-permute-start(f32[1,260,2]{2,1,0:T(8,128)S(1)} %get-tuple-element.57), channel_id=1, source_target_pairs={{8,0},{16,8},{24,16},{0,24},{9,1},{17,9},{25,17},{1,25},{10,2},{18... | collective-permute-start | bytes 6248 | tf_op jit(solution)/shard_map/ppermute | solution.py:23
  177.5 6.7 %collective-permute-start.27 = (f32[1,260,2]{2,1,0:T(8,128)S(1)}, f32[1,260,2]{2,1,0:T(8,128)S(1)}, u32[]{:S(2)}, u32[]{:S(2)}) collective-permute-start(f32[1,260,2]{2,1,0:T(8,128)S(1)} %get-tuple-element.58), channel_id=1, source_target_pairs={{0,8},{8,16},{16,24},{24,0},{1,9},{9,17},{17,25},{25,1},{2,10},{10... | collective-permute-start | bytes 6248 | tf_op jit(solution)/shard_map/ppermute | solution.py:20
  185.0 4.9 %collective-permute-start.28 = (f32[1,2,1024]{2,1,0:T(2,128)S(1)}, f32[1,2,1024]{2,1,0:T(2,128)S(1)}, u32[]{:S(2)}, u32[]{:S(2)}) collective-permute-start(f32[1,2,1024]{2,1,0:T(2,128)S(1)} %get-tuple-element.86), channel_id=1, source_target_pairs={{0,1},{1,2},{2,3},{3,4},{4,5},{5,6},{6,7},{7,0},{8,9},{9,10},{10,1... | collective-permute-start | bytes 24584 | tf_op jit(solution)/shard_map/ppermute | solution.py:20
  190.1 6.2 %collective-permute-start.30 = (f32[1,260,2]{2,1,0:T(8,128)S(1)}, f32[1,260,2]{2,1,0:T(8,128)S(1)}, u32[]{:S(2)}, u32[]{:S(2)}) collective-permute-start(f32[1,260,2]{2,1,0:T(8,128)S(1)} %get-tuple-element.55), channel_id=1, source_target_pairs={{8,0},{16,8},{24,16},{0,24},{9,1},{17,9},{25,17},{1,25},{10,2},{18... | collective-permute-start | bytes 6248 | tf_op jit(solution)/shard_map/ppermute | solution.py:23
  191.3 6.0 %collective-permute-start.31 = (f32[1,260,2]{2,1,0:T(8,128)S(1)}, f32[1,260,2]{2,1,0:T(8,128)S(1)}, u32[]{:S(2)}, u32[]{:S(2)}) collective-permute-start(f32[1,260,2]{2,1,0:T(8,128)S(1)} %get-tuple-element.56), channel_id=1, source_target_pairs={{0,8},{8,16},{16,24},{24,0},{1,9},{9,17},{17,25},{25,1},{2,10},{10... | collective-permute-start | bytes 6248 | tf_op jit(solution)/shard_map/ppermute | solution.py:20
  200.7 4.9 %collective-permute-start.32 = (f32[1,2,1024]{2,1,0:T(2,128)S(1)}, f32[1,2,1024]{2,1,0:T(2,128)S(1)}, u32[]{:S(2)}, u32[]{:S(2)}) collective-permute-start(f32[1,2,1024]{2,1,0:T(2,128)S(1)} %get-tuple-element.84), channel_id=1, source_target_pairs={{0,1},{1,2},{2,3},{3,4},{4,5},{5,6},{6,7},{7,0},{8,9},{9,10},{10,1... | collective-permute-start | bytes 24584 | tf_op jit(solution)/shard_map/ppermute | solution.py:20
  205.8 5.8 %collective-permute-start.34 = (f32[1,260,2]{2,1,0:T(8,128)S(1)}, f32[1,260,2]{2,1,0:T(8,128)S(1)}, u32[]{:S(2)}, u32[]{:S(2)}) collective-permute-start(f32[1,260,2]{2,1,0:T(8,128)S(1)} %get-tuple-element.53), channel_id=1, source_target_pairs={{8,0},{16,8},{24,16},{0,24},{9,1},{17,9},{25,17},{1,25},{10,2},{18... | collective-permute-start | bytes 6248 | tf_op jit(solution)/shard_map/ppermute | solution.py:23
  208.0 5.9 %collective-permute-start.35 = (f32[1,260,2]{2,1,0:T(8,128)S(1)}, f32[1,260,2]{2,1,0:T(8,128)S(1)}, u32[]{:S(2)}, u32[]{:S(2)}) collective-permute-start(f32[1,260,2]{2,1,0:T(8,128)S(1)} %get-tuple-element.54), channel_id=1, source_target_pairs={{0,8},{8,16},{16,24},{24,0},{1,9},{9,17},{17,25},{25,1},{2,10},{10... | collective-permute-start | bytes 6248 | tf_op jit(solution)/shard_map/ppermute | solution.py:20
  214.8 4.9 %collective-permute-start.36 = (f32[1,2,1024]{2,1,0:T(2,128)S(1)}, f32[1,2,1024]{2,1,0:T(2,128)S(1)}, u32[]{:S(2)}, u32[]{:S(2)}) collective-permute-start(f32[1,2,1024]{2,1,0:T(2,128)S(1)} %get-tuple-element.82), channel_id=1, source_target_pairs={{0,1},{1,2},{2,3},{3,4},{4,5},{5,6},{6,7},{7,0},{8,9},{9,10},{10,1... | collective-permute-start | bytes 24584 | tf_op jit(solution)/shard_map/ppermute | solution.py:20
  219.9 5.8 %collective-permute-start.38 = (f32[1,260,2]{2,1,0:T(8,128)S(1)}, f32[1,260,2]{2,1,0:T(8,128)S(1)}, u32[]{:S(2)}, u32[]{:S(2)}) collective-permute-start(f32[1,260,2]{2,1,0:T(8,128)S(1)} %get-tuple-element.51), channel_id=1, source_target_pairs={{8,0},{16,8},{24,16},{0,24},{9,1},{17,9},{25,17},{1,25},{10,2},{18... | collective-permute-start | bytes 6248 | tf_op jit(solution)/shard_map/ppermute | solution.py:23
  220.8 7.1 %collective-permute-start.39 = (f32[1,260,2]{2,1,0:T(8,128)S(1)}, f32[1,260,2]{2,1,0:T(8,128)}, u32[]{:S(2)}, u32[]{:S(2)}) collective-permute-start(f32[1,260,2]{2,1,0:T(8,128)S(1)} %get-tuple-element.52), channel_id=1, source_target_pairs={{0,8},{8,16},{16,24},{24,0},{1,9},{9,17},{17,25},{25,1},{2,10},{10... | collective-permute-start | bytes 6248 | tf_op jit(solution)/shard_map/ppermute | solution.py:20
  277.6 5.0 %collective-permute-start.40 = (f32[1,2,1024]{2,1,0:T(2,128)S(1)}, f32[1,2,1024]{2,1,0:T(2,128)S(1)}, u32[]{:S(2)}, u32[]{:S(2)}) collective-permute-start(f32[1,2,1024]{2,1,0:T(2,128)S(1)} %get-tuple-element.80), channel_id=1, source_target_pairs={{0,1},{1,2},{2,3},{3,4},{4,5},{5,6},{6,7},{7,0},{8,9},{9,10},{10,1... | collective-permute-start | bytes 24584 | tf_op jit(solution)/shard_map/ppermute | solution.py:20
  277.7 4.9 %collective-permute-start.41 = (f32[1,2,1024]{2,1,0:T(2,128)S(1)}, f32[1,2,1024]{2,1,0:T(2,128)S(1)}, u32[]{:S(2)}, u32[]{:S(2)}) collective-permute-start(f32[1,2,1024]{2,1,0:T(2,128)S(1)} %get-tuple-element.79), channel_id=1, source_target_pairs={{1,0},{2,1},{3,2},{4,3},{5,4},{6,5},{7,6},{0,7},{9,8},{10,9},{11,1... | collective-permute-start | bytes 24584 | tf_op jit(solution)/shard_map/ppermute | solution.py:23
  282.8 6.5 %collective-permute-start.42 = (f32[1,260,2]{2,1,0:T(8,128)S(1)}, f32[1,260,2]{2,1,0:T(8,128)S(1)}, u32[]{:S(2)}, u32[]{:S(2)}) collective-permute-start(f32[1,260,2]{2,1,0:T(8,128)S(1)} %get-tuple-element.49), channel_id=1, source_target_pairs={{8,0},{16,8},{24,16},{0,24},{9,1},{17,9},{25,17},{1,25},{10,2},{18... | collective-permute-start | bytes 6248 | tf_op jit(solution)/shard_map/ppermute | solution.py:23
  285.1 8.0 %collective-permute-start.43 = (f32[1,260,2]{2,1,0:T(8,128)S(1)}, f32[1,260,2]{2,1,0:T(8,128)S(1)}, u32[]{:S(2)}, u32[]{:S(2)}) collective-permute-start(f32[1,260,2]{2,1,0:T(8,128)S(1)} %get-tuple-element.50), channel_id=1, source_target_pairs={{0,8},{8,16},{16,24},{24,0},{1,9},{9,17},{17,25},{25,1},{2,10},{10... | collective-permute-start | bytes 6248 | tf_op jit(solution)/shard_map/ppermute | solution.py:20
  294.0 4.9 %collective-permute-start.44 = (f32[1,2,1024]{2,1,0:T(2,128)S(1)}, f32[1,2,1024]{2,1,0:T(2,128)S(1)}, u32[]{:S(2)}, u32[]{:S(2)}) collective-permute-start(f32[1,2,1024]{2,1,0:T(2,128)S(1)} %get-tuple-element.78), channel_id=1, source_target_pairs={{0,1},{1,2},{2,3},{3,4},{4,5},{5,6},{6,7},{7,0},{8,9},{9,10},{10,1... | collective-permute-start | bytes 24584 | tf_op jit(solution)/shard_map/ppermute | solution.py:20
  299.1 6.1 %collective-permute-start.46 = (f32[1,260,2]{2,1,0:T(8,128)S(1)}, f32[1,260,2]{2,1,0:T(8,128)S(1)}, u32[]{:S(2)}, u32[]{:S(2)}) collective-permute-start(f32[1,260,2]{2,1,0:T(8,128)S(1)} %get-tuple-element.47), channel_id=1, source_target_pairs={{8,0},{16,8},{24,16},{0,24},{9,1},{17,9},{25,17},{1,25},{10,2},{18... | collective-permute-start | bytes 6248 | tf_op jit(solution)/shard_map/ppermute | solution.py:23
  300.4 6.2 %collective-permute-start.47 = (f32[1,260,2]{2,1,0:T(8,128)S(1)}, f32[1,260,2]{2,1,0:T(8,128)S(1)}, u32[]{:S(2)}, u32[]{:S(2)}) collective-permute-start(f32[1,260,2]{2,1,0:T(8,128)S(1)} %get-tuple-element.48), channel_id=1, source_target_pairs={{0,8},{8,16},{16,24},{24,0},{1,9},{9,17},{17,25},{25,1},{2,10},{10... | collective-permute-start | bytes 6248 | tf_op jit(solution)/shard_map/ppermute | solution.py:20
  309.9 4.9 %collective-permute-start.48 = (f32[1,2,1024]{2,1,0:T(2,128)S(1)}, f32[1,2,1024]{2,1,0:T(2,128)S(1)}, u32[]{:S(2)}, u32[]{:S(2)}) collective-permute-start(f32[1,2,1024]{2,1,0:T(2,128)S(1)} %get-tuple-element.76), channel_id=1, source_target_pairs={{0,1},{1,2},{2,3},{3,4},{4,5},{5,6},{6,7},{7,0},{8,9},{9,10},{10,1... | collective-permute-start | bytes 24584 | tf_op jit(solution)/shard_map/ppermute | solution.py:20
  315.0 6.2 %collective-permute-start.50 = (f32[1,260,2]{2,1,0:T(8,128)S(1)}, f32[1,260,2]{2,1,0:T(8,128)S(1)}, u32[]{:S(2)}, u32[]{:S(2)}) collective-permute-start(f32[1,260,2]{2,1,0:T(8,128)S(1)} %get-tuple-element.45), channel_id=1, source_target_pairs={{8,0},{16,8},{24,16},{0,24},{9,1},{17,9},{25,17},{1,25},{10,2},{18... | collective-permute-start | bytes 6248 | tf_op jit(solution)/shard_map/ppermute | solution.py:23
  316.9 6.2 %collective-permute-start.51 = (f32[1,260,2]{2,1,0:T(8,128)S(1)}, f32[1,260,2]{2,1,0:T(8,128)S(1)}, u32[]{:S(2)}, u32[]{:S(2)}) collective-permute-start(f32[1,260,2]{2,1,0:T(8,128)S(1)} %get-tuple-element.46), channel_id=1, source_target_pairs={{0,8},{8,16},{16,24},{24,0},{1,9},{9,17},{17,25},{25,1},{2,10},{10... | collective-permute-start | bytes 6248 | tf_op jit(solution)/shard_map/ppermute | solution.py:20
  323.9 4.9 %collective-permute-start.52 = (f32[1,2,1024]{2,1,0:T(2,128)S(1)}, f32[1,2,1024]{2,1,0:T(2,128)S(1)}, u32[]{:S(2)}, u32[]{:S(2)}) collective-permute-start(f32[1,2,1024]{2,1,0:T(2,128)S(1)} %get-tuple-element.74), channel_id=1, source_target_pairs={{0,1},{1,2},{2,3},{3,4},{4,5},{5,6},{6,7},{7,0},{8,9},{9,10},{10,1... | collective-permute-start | bytes 24584 | tf_op jit(solution)/shard_map/ppermute | solution.py:20
  329.0 5.3 %collective-permute-start.54 = (f32[1,260,2]{2,1,0:T(8,128)S(1)}, f32[1,260,2]{2,1,0:T(8,128)S(1)}, u32[]{:S(2)}, u32[]{:S(2)}) collective-permute-start(f32[1,260,2]{2,1,0:T(8,128)S(1)} %get-tuple-element.43), channel_id=1, source_target_pairs={{8,0},{16,8},{24,16},{0,24},{9,1},{17,9},{25,17},{1,25},{10,2},{18... | collective-permute-start | bytes 6248 | tf_op jit(solution)/shard_map/ppermute | solution.py:23
  330.4 5.9 %collective-permute-start.55 = (f32[1,260,2]{2,1,0:T(8,128)S(1)}, f32[1,260,2]{2,1,0:T(8,128)S(1)}, u32[]{:S(2)}, u32[]{:S(2)}) collective-permute-start(f32[1,260,2]{2,1,0:T(8,128)S(1)} %get-tuple-element.44), channel_id=1, source_target_pairs={{0,8},{8,16},{16,24},{24,0},{1,9},{9,17},{17,25},{25,1},{2,10},{10... | collective-permute-start | bytes 6248 | tf_op jit(solution)/shard_map/ppermute | solution.py:20
  385.4 7.3 %collective-permute-start.58 = (f32[1,258,1]{2,1,0:T(8,128)S(1)}, f32[1,258,1]{2,1,0:T(8,128)S(1)}, u32[]{:S(2)}, u32[]{:S(2)}) collective-permute-start(f32[1,258,1]{2,1,0:T(8,128)S(1)} %get-tuple-element.69), channel_id=1, source_target_pairs={{8,0},{16,8},{24,16},{0,24},{9,1},{17,9},{25,17},{1,25},{10,2},{18... | collective-permute-start | bytes 3104 | tf_op jit(solution)/shard_map/ppermute | solution.py:23
  388.8 7.1 %collective-permute-start.59 = (f32[1,258,1]{2,1,0:T(8,128)S(1)}, f32[1,258,1]{2,1,0:T(8,128)S(1)}, u32[]{:S(2)}, u32[]{:S(2)}) collective-permute-start(f32[1,258,1]{2,1,0:T(8,128)S(1)} %get-tuple-element.70), channel_id=1, source_target_pairs={{0,8},{8,16},{16,24},{24,0},{1,9},{9,17},{17,25},{25,1},{2,10},{10... | collective-permute-start | bytes 3104 | tf_op jit(solution)/shard_map/ppermute | solution.py:20
  (34 other events, 478.1 us)
where the time goes:
time: 399 us; the launch traced here: 398 us
  waiting for transfers between devices  123 us (31%)
  blocking collectives  116 us (29%)
  starting transfers between devices  91.2 us (23%)
  other arithmetic  41.2 us (10%)
  local copies, waits for them, and re-layouts  14.6 us (4%)
  between operations  11.9 us (3%)
    psum x3, blocking collectives, joint_products(): lax.psum((local_sum(residual * precond), local_sum(precond * product)), (...  116 us
    ppermute x30, starting transfers between devices, extended(): lax.ppermute(lax.slice_in_dim(block, 0, width, axis=dim), axis, backward)  79.2 us
    ppermute x30, waiting for transfers between devices, extended(): lax.ppermute(lax.slice_in_dim(block, block.shape[dim] - width, None, axis...  65.4 us
    ppermute x30, waiting for transfers between devices, extended(): lax.ppermute(lax.slice_in_dim(block, 0, width, axis=dim), axis, backward)  57.9 us
    add x9, other arithmetic, chebyshev(): approx = approx + update  15.4 us
    ppermute x30, starting transfers between devices, extended(): lax.ppermute(lax.slice_in_dim(block, block.shape[dim] - width, None, axis...  12 us
    div x3, other arithmetic, chebyshev(): update = residual / center  8.98 us
    concatenate x2, local copies, waits for them, and re-layouts, extended(): block = jnp.concatenate([low, block, high], axis=dim)  8.68 us
  transfers between devices with their start and end apart: 60, of which 46 were waited for; matrix products, arithmetic and copies ran while one was open for 0% of the time, Pallas kernels for 0%

commit v1 on v0

v1 whole, which is shorter than its diff:
```python
import functools

import jax
import jax.numpy as jnp
from jax import lax
from jax.experimental import pallas as pl
from jax.experimental.pallas import tpu as pltpu
from jax.sharding import PartitionSpec as P

HALO = 32
LANES = 128
SUB = 8
MESH = pl.DeviceIdType.MESH

advect_courant = 0.2
implicit_weight = 0.25
explicit_weight = 0.5


def preconditioner_polynomial(stiff):
    one = jnp.ones_like(stiff)
    upper = 1.0 + 2.0 * stiff
    center = (upper + 1.0) * 0.5
    half = (upper - 1.0) * 0.5
    ratio = center / half
    sigma = stiff * 0.25
    rho = 1.0 / ratio
    update = [1.0 / center]
    approx = list(update)
    for _ in range(3):
        misfit = [one] + [jnp.zeros_like(stiff)] * len(approx)
        for k, value in enumerate(approx):
            misfit[k] = misfit[k] - center * value
            misfit[k + 1] = misfit[k + 1] + sigma * value
        rho_next = 1.0 / (2.0 * ratio - rho)
        first = rho_next * rho
        second = 2.0 * rho_next / half
        update = [
            (first * update[k] if k < len(update) else 0.0) + second * misfit[k]
            for k in range(len(misfit))
        ]
        approx = [
            (approx[k] if k < len(approx) else 0.0) + update[k] for k in range(len(update))
        ]
        rho = rho_next
    return approx, center, sigma


def kernel(
    nx, ny, rows, tiles,
    wave_ref, h_in, u_in, v_in, x_out, u_out, v_out,
    fields, su, sv, src, tmp_a, tmp_b, z0, q0, m0, n0, m1, n1,
    row_halo, pack, pack_halo, stage,
    red_send, red_gy, red_gx,
    load_sem, row_ss, row_rs, col_ss, col_rs,
    gy_ss, gy_rs, gx_ss, gx_rs, out_sem,
):
    gx = lax.axis_index("gx")
    gy = lax.axis_index("gy")
    right, left = lax.rem(gx + 1, nx), lax.rem(gx + nx - 1, nx)
    high, low = lax.rem(gy + 1, ny), lax.rem(gy + ny - 1, ny)
    width = tiles * LANES
    ring = tiles + 1
    inputs = (h_in, u_in, v_in)

    barrier = pltpu.get_barrier_semaphore()
    greeted = [{"gy": lax.rem(gy + o, ny)} for o in range(1, ny)]
    greeted += [{"gx": lax.rem(gx + o, nx)} for o in range(1, nx)]
    greeted += [{"gx": a, "gy": b} for a in (left, right) for b in (low, high)]
    for device in greeted:
        pl.semaphore_signal(barrier, inc=1, device_id=device, device_id_type=MESH)

    loads = {}
    for c in [0, tiles - 1] + list(range(1, tiles - 1)):
        for f in range(3):
            loads[f, c] = pltpu.make_async_copy(
                inputs[f].at[0, :, pl.ds(c * LANES, LANES)],
                fields.at[f, c, pl.ds(HALO, rows), :],
                load_sem.at[f, c],
            )
            loads[f, c].start()
    pl.semaphore_wait(barrier, len(greeted))

    row_copies = []
    for f in range(3):
        for side, device, first in ((0, high, rows - HALO), (1, low, 0)):
            row_copies.append(
                pltpu.make_async_remote_copy(
                    src_ref=inputs[f].at[0, pl.ds(first, HALO), :],
                    dst_ref=row_halo.at[side, f],
                    send_sem=row_ss.at[side, f],
                    recv_sem=row_rs.at[side, f],
                    device_id={"gy": device},
                    device_id_type=MESH,
                )
            )
            row_copies[-1].start()

    lane = lax.broadcasted_iota(jnp.int32, (SUB, LANES), 1)

    for f in range(3):
        loads[f, 0].wait()
        loads[f, tiles - 1].wait()
    for f in range(3):
        def pack_group(g, carry, f=f):
            for side, tile, at in ((0, tiles - 1, LANES - HALO), (1, 0, 0)):
                packed = None
                for j in range(4):
                    start = pl.multiple_of(HALO + g * 32 + j * SUB, SUB)
                    value = fields[f, tile, pl.ds(start, SUB), :]
                    shift = (j * 32 - at) % LANES
                    if shift:
                        value = pltpu.roll(value, shift, 1)
                    packed = value if packed is None else jnp.where(lane < j * 32, packed, value)
                pack[side, f, pl.ds(pl.multiple_of(g * SUB, SUB), SUB), :] = packed
            return carry

        lax.fori_loop(0, rows // 32, pack_group, 0)
    deep = rows // 4
    col_copies = []
    for side, device in ((0, right), (1, left)):
        for part, target, first, size, dest in (
            (0, {"gx": device}, 0, deep, SUB),
            (1, {"gx": device, "gy": high}, deep - SUB, SUB, 0),
            (2, {"gx": device, "gy": low}, 0, SUB, deep + SUB),
        ):
            col_copies.append(
                pltpu.make_async_remote_copy(
                    src_ref=pack.at[side, :, pl.ds(first, size), :],
                    dst_ref=pack_halo.at[side, :, pl.ds(dest, size), :],
                    send_sem=col_ss.at[side, part],
                    recv_sem=col_rs.at[side, part],
                    device_id=target,
                    device_id_type=MESH,
                )
            )
            col_copies[-1].start()

    wave = jnp.full((SUB, LANES), wave_ref[0], jnp.float32) * implicit_weight
    stiff = wave * wave
    coef, center, sigma = preconditioner_polynomial(stiff)

    for c in range(1, tiles - 1):
        for f in range(3):
            loads[f, c].wait()
    for copy in row_copies:
        copy.wait()
    for f in range(3):
        for c in range(tiles):
            cols = pl.ds(c * LANES, LANES)
            fields[f, c, pl.ds(0, HALO), :] = row_halo[0, f, :, cols]
            fields[f, c, pl.ds(HALO + rows, HALO), :] = row_halo[1, f, :, cols]
    for copy in col_copies:
        copy.wait()
    for f in range(3):
        def unpack_group(g, carry, f=f):
            at = pl.ds(pl.multiple_of(g * SUB, SUB), SUB)
            from_left = pack_halo[0, f, at, :]
            from_right = pack_halo[1, f, at, :]
            for j in range(4):
                shift_r = (-j * 32) % LANES
                shift_l = (LANES - HALO - j * 32) % LANES
                a = pltpu.roll(from_right, shift_r, 1) if shift_r else from_right
                b = pltpu.roll(from_left, shift_l, 1) if shift_l else from_left
                start = pl.multiple_of(g * 32 + j * SUB, SUB)
                fields[f, tiles, pl.ds(start, SUB), :] = jnp.where(lane < 64, a, b)
            return carry

        lax.fori_loop(0, (rows + 2 * HALO) // 32, unpack_group, 0)

    def lane_pairs(values, distance):
        to_right = [pltpu.roll(v, distance, 1) for v in values]
        to_left = [pltpu.roll(v, LANES - distance, 1) for v in values]
        from_left = [
            jnp.where(lane < distance, to_right[c - 1], to_right[c]) for c in range(len(values))
        ]
        from_right = [
            jnp.where(lane >= LANES - distance, to_left[(c + 1) % len(values)], to_left[c])
            for c in range(len(values))
        ]
        return from_left, from_right

    factor = explicit_weight * advect_courant
    half_wave = 0.5 * wave

    def section(i, carry):
        base = pl.multiple_of(i * SUB, SUB)
        at, up, down = (pl.ds(base + k, SUB) for k in (7, 6, 8))
        h = [fields[0, c, at, :] for c in range(ring)]
        u = [fields[1, c, at, :] for c in range(ring)]
        v = [fields[2, c, at, :] for c in range(ring)]
        sides = [lane_pairs(q, 1) for q in (h, u, v)]
        for c in range(ring):
            east = u[c] > 0
            north = v[c] > 0
            fu = factor * u[c]
            fv = factor * v[c]
            moved = []
            grads = []
            for f, q in enumerate((h, u, v)):
                w, e = sides[f][0][c], sides[f][1][c]
                s, n = fields[f, c, up, :], fields[f, c, down, :]
                mid = q[c]
                moved.append(
                    mid
                    - (
                        fu * jnp.where(east, mid - w, e - mid)
                        + fv * jnp.where(north, mid - s, n - mid)
                    )
                )
                grads.append((e - w, n - s))
            src[c, at, :] = moved[0] - half_wave * (grads[1][0] + grads[2][1])
            su[c, at, :] = moved[1] - half_wave * grads[0][0]
            sv[c, at, :] = moved[2] - half_wave * grads[0][1]
        return carry

    lax.fori_loop(0, (rows + 2 * HALO) // SUB - 1, section, 0)

    def source(i, carry):
        base = pl.multiple_of(i * SUB, SUB)
        at, up, down = (pl.ds(base + k, SUB) for k in (0, -1, 1))
        w, e = lane_pairs([su[c, at, :] for c in range(ring)], 1)
        for c in range(ring):
            grad = (e[c] - w[c]) + (sv[c, down, :] - sv[c, up, :])
            src[c, at, :] = src[c, at, :] - half_wave * grad
        return carry

    lax.fori_loop(1, (rows + 2 * HALO) // SUB - 1, source, 0)

    def neighbour_sums(ref, base):
        mids = [ref[c, pl.ds(base, SUB), :] for c in range(ring)]
        w, e = lane_pairs(mids, 2)
        sums = [
            (w[c] + e[c]) + (ref[c, pl.ds(base - 2, SUB), :] + ref[c, pl.ds(base + 2, SUB), :])
            for c in range(ring)
        ]
        return mids, sums

    def stencil(step, ref, out, combine):
        valid = 24 - 2 * step
        lo = (HALO - valid) // SUB
        hi = -(-(HALO + rows + valid) // SUB)

        def body(i, carry):
            base = pl.multiple_of(i * SUB, SUB)
            mids, sums = neighbour_sums(ref, base)
            for c in range(ring):
                out[c, pl.ds(base, SUB), :] = combine(c, base, mids[c], sums[c])
            return carry

        lax.fori_loop(lo, hi, body, 0)

    def precondition_half(step, r, z, first):
        at = lambda c, base: r[c, pl.ds(base, SUB), :]
        if first:
            stencil(step, r, tmp_a, lambda c, b, mid, s: coef[2] * mid + coef[3] * s)
            stencil(step + 1, tmp_a, tmp_b, lambda c, b, mid, s: coef[1] * at(c, b) + s)
        else:
            stencil(step, tmp_b, z, lambda c, b, mid, s: coef[0] * at(c, b) + s)

    def operator(step, z, q):
        stencil(step, z, q, lambda c, b, mid, s: center * mid - sigma * s)

    def dots(index, load):
        def body(i, carry):
            first, second = carry
            base = pl.multiple_of(HALO + i * SUB, SUB)
            for c in range(tiles):
                r, z, w = load(lambda ref: ref[c, pl.ds(base, SUB), :])
                first[c % 2] = first[c % 2] + r * z
                second[c % 2] = second[c % 2] + z * w
            return first, second

        zero = jnp.zeros((SUB, LANES), jnp.float32)
        first, second = lax.fori_loop(
            0, rows // SUB, body, ([zero, zero], [zero, zero])
        )
        red_send[index, 0, pl.ds(0, 1), :] = jnp.sum(first[0] + first[1], axis=0, keepdims=True)
        red_send[index, 0, pl.ds(1, 1), :] = jnp.sum(second[0] + second[1], axis=0, keepdims=True)

    def gather(index, phase):
        count, axis, me = ((ny, "gy", gy), (nx, "gx", gx))[phase]
        slots, ss, rs = ((red_gy, gy_ss, gy_rs), (red_gx, gx_ss, gx_rs))[phase]
        copies = []
        for o in range(1, count):
            copies.append(
                pltpu.make_async_remote_copy(
                    src_ref=red_send.at[index, phase],
                    dst_ref=slots.at[index, o],
                    send_sem=ss.at[index, o],
                    recv_sem=rs.at[index, o],
                    device_id={axis: lax.rem(me + o, count)},
                    device_id_type=MESH,
                )
            )
            copies[-1].start()
        return copies

    def gathered(index, phase, copies):
        slots = (red_gy, red_gx)[phase]
        for copy in copies:
            copy.wait()
        total = red_send[index, phase]
        for o in range(1, len(copies) + 1):
            total = total + slots[index, o]
        return total

    def totals(index, copies):
        total = gathered(index, 1, copies)
        sums = jnp.sum(total, axis=1, keepdims=True)
        full = jnp.broadcast_to(sums, (SUB, LANES))
        return (
            jnp.broadcast_to(full[0:1, :], (SUB, LANES)),
            jnp.broadcast_to(full[1:2, :], (SUB, LANES)),
        )

    def first_phase(index, load):
        red_send[index, 0] = jnp.zeros((SUB, LANES), jnp.float32)
        dots(index, load)
        return gather(index, 0)

    def second_phase(index, copies):
        red_send[index, 1] = gathered(index, 0, copies)
        return gather(index, 1)

    precondition_half(1, src, z0, True)
    precondition_half(3, src, z0, False)
    operator(4, z0, q0)
    copies = first_phase(0, lambda get: (get(src), get(z0), get(q0)))
    precondition_half(5, q0, m0, True)
    copies = second_phase(0, copies)
    precondition_half(7, q0, m0, False)
    operator(8, m0, n0)
    rz0, zw0 = totals(0, copies)
    alpha0 = rz0 / zw0

    copies = first_phase(
        1,
        lambda get: (
            get(src) - alpha0 * get(q0),
            get(z0) - alpha0 * get(m0),
            get(q0) - alpha0 * get(n0),
        ),
    )
    precondition_half(9, n0, m1, True)
    copies = second_phase(1, copies)
    precondition_half(11, n0, m1, False)
    operator(12, m1, n1)
    rz1, zw1 = totals(1, copies)
    beta1 = rz1 / rz0
    alpha1 = rz1 / (zw1 - beta1 * rz1 / alpha0)

    linear = alpha0 + alpha1 * (1.0 + beta1)
    square = alpha0 * alpha1
    copies = first_phase(
        2,
        lambda get: (
            get(src) - linear * get(q0) + square * get(n0),
            get(z0) - linear * get(m0) + square * get(m1),
            get(q0) - linear * get(n0) + square * get(n1),
        ),
    )
    copies = second_phase(2, copies)
    rz2, zw2 = totals(2, copies)
    beta2 = rz2 / rz1
    alpha2 = rz2 / (zw2 - beta2 * rz2 / alpha1)

    along = alpha1 + alpha2 * beta2
    take_z0 = alpha0 + along * (1.0 + beta1) + alpha2
    take_m0 = -(along * alpha0 + alpha2 * linear)
    take_m1 = alpha2 * square

    solved = tmp_a

    def combine(i, carry):
        base = pl.multiple_of(i * SUB, SUB)
        at = pl.ds(base, SUB)
        for c in range(ring):
            solved[c, at, :] = take_z0 * z0[c, at, :] + take_m0 * m0[c, at, :] + take_m1 * m1[c, at, :]
        return carry

    lax.fori_loop(HALO // SUB - 1, (HALO + rows) // SUB + 1, combine, 0)

    outputs = (x_out, u_out, v_out)
    chunks = 4
    chunk = rows // chunks
    writes = []
    for k in range(chunks):
        def finish(i, carry, k=k):
            base = pl.multiple_of(HALO + k * chunk + i * SUB, SUB)
            to = pl.ds(pl.multiple_of(k * chunk + i * SUB, SUB), SUB)
            mids = [solved[c, pl.ds(base, SUB), :] for c in range(ring)]
            w, e = lane_pairs(mids, 1)
            for c in range(tiles):
                at = pl.ds(base, SUB)
                cols = pl.ds(c * LANES, LANES)
                north = solved[c, pl.ds(base + 1, SUB), :]
                south = solved[c, pl.ds(base - 1, SUB), :]
                stage[0, to, cols] = mids[c]
                stage[1, to, cols] = su[c, at, :] - half_wave * (e[c] - w[c])
                stage[2, to, cols] = sv[c, at, :] - half_wave * (north - south)
            return carry

        lax.fori_loop(0, chunk // SUB, finish, 0)
        for f in range(3):
            part = pl.ds(k * chunk, chunk)
            writes.append(
                pltpu.make_async_copy(
                    stage.at[f, part, :], outputs[f].at[0, part, :], out_sem.at[f, k]
                )
            )
            writes[-1].start()
    for copy in writes:
        copy.wait()


def local(mesh, height, zonal_velocity, meridional_velocity, wave_courant):
    nx, ny = mesh.shape["gx"], mesh.shape["gy"]
    _, rows, width = height.shape
    tiles = width // LANES
    extended = (tiles + 1, rows + 2 * HALO, LANES)
    f32 = jnp.float32
    dma = pltpu.SemaphoreType.DMA
    hbm = pl.BlockSpec(memory_space=pl.ANY)
    out = jax.ShapeDtypeStruct(height.shape, f32)
    return pl.pallas_call(
        functools.partial(kernel, nx, ny, rows, tiles),
        out_shape=(out, out, out),
        in_specs=[pl.BlockSpec(memory_space=pltpu.SMEM), hbm, hbm, hbm],
        out_specs=(hbm, hbm, hbm),
        scratch_shapes=[pltpu.VMEM((3,) + extended, f32)]
        + [pltpu.VMEM(extended, f32)] * 11
        + [
            pltpu.VMEM((2, 3, HALO, width), f32),
            pltpu.VMEM((2, 3, rows // 4, LANES), f32),
            pltpu.VMEM((2, 3, rows // 4 + 2 * SUB, LANES), f32),
            pltpu.VMEM((3, rows, width), f32),
            pltpu.VMEM((3, 2, SUB, LANES), f32),
            pltpu.VMEM((3, ny, SUB, LANES), f32),
            pltpu.VMEM((3, nx, SUB, LANES), f32),
            dma((3, tiles)),
            dma((2, 3)),
            dma((2, 3)),
            dma((2, 3)),
            dma((2, 3)),
            dma((3, ny)),
            dma((3, ny)),
            dma((3, nx)),
            dma((3, nx)),
            dma((3, 4)),
        ],
        compiler_params=pltpu.CompilerParams(
            collective_id=0, has_side_effects=True, vmem_limit_bytes=56 * 1024 * 1024
        ),
    )(wave_courant, height, zonal_velocity, meridional_velocity)


def solution(mesh):
    spec = P(None, "gy", "gx")
    return jax.shard_map(
        functools.partial(local, mesh),
        mesh=mesh,
        in_specs=(spec, spec, spec, P()),
        out_specs=(spec, spec, spec),
        check_vma=False,
    )
```

time: 399 us -> 90.5 us (0.23)
  waiting for transfers between devices: 123 us -> 0 us
  blocking collectives: 116 us -> 0 us
  starting transfers between devices: 91.2 us -> 0 us
  Pallas kernels: 0 us -> 84 us
  other arithmetic: 41.2 us -> 0 us
  between operations: 11.9 us -> 1.3 us
  local copies, waits for them, and re-layouts: 14.6 us -> 4.97 us
    ppermute x60 -> x0, waiting for transfers between devices: 123 us -> none  [the longest x30 65.4 us: extended(): lax.ppermute(lax.slice_in_dim(block, block.shape[dim] - width, None, axis...]
    psum x3 -> x0, blocking collectives: 116 us -> none  [joint_products(): lax.psum((local_sum(residual * precond), local_sum(precond * product)), (...]
    ppermute x60 -> x0, starting transfers between devices: 91.2 us -> none  [the longest x30 79.2 us: extended(): lax.ppermute(lax.slice_in_dim(block, 0, width, axis=dim), axis, backward)]
    pallas_call x0 -> x1, Pallas kernels: none -> 84 us  [local(): pl.pallas_call(functools.partial(kernel, nx, ny, rows, tiles), out_shape=...]
    add x10 -> x0, other arithmetic: 15.8 us -> none  [the longest x9 15.4 us: chebyshev(): approx = approx + update]
    div x3 -> x0, other arithmetic: 8.98 us -> none  [chebyshev(): update = residual / center]
    concatenate x2 -> x0, local copies, waits for them, and re-layouts: 8.68 us -> none  [extended(): block = jnp.concatenate([low, block, high], axis=dim)]
    sub x3 -> x0, other arithmetic: 6.17 us -> none  [the longest x1 2.13 us: local(): section_meridional - wave_factor * centered_meridional(solved_pad)]
  transfers between devices with their start and end apart: 60 -> 0, of which waited for: 46 -> 0; matrix products, arithmetic and copies ran while one was open for 0% -> 0% of each run, Pallas kernels for 0% -> 0%
where the time goes in v1:
time: 90.5 us; the launch traced here: 90.3 us
  Pallas kernels  84 us (93%)
  local copies, waits for them, and re-layouts  4.97 us (5%)
  between operations  1.3 us (1%)
    pallas_call x1, Pallas kernels, local(): pl.pallas_call(functools.partial(kernel, nx, ny, rows, tiles), out_shape=...  84 us
    unnamed x7, local copies, waits for them, and re-layouts  4.97 us

profile of v1, /device:TPU:0, one launch (start us, length us, event | category | flops | bytes accessed | tf_op | source)
XLA Modules:
  0.0 90.3 jit_solution(1023349362906268773)
XLA Ops:
  1.3 84.0 %shard_map.67 = (f32[1,256,1024]{2,1,0:T(8,128)}, f32[1,256,1024]{2,1,0:T(8,128)}, f32[1,256,1024]{2,1,0:T(8,128)}) custom-call(f32[1]{0:T(128)S(6)} %copy.10.wave_ref, f32[1,256,1024]{2,1,0:T(8,128)} %h_in.1, f32[1,256,1024]{2,1,0:T(8,128)} %u_in.1, f32[1,256,1024]{2,1,0:T(8,128)} %v_in.1), custom_call_target="tpu_custom_call" | custom-call | tf_op jit(solution)/shard_map/pallas_call | solution.py:426
  85.3 0.0 copy-start.1
  85.3 2.4 %copy.11 = f32[1,256,1024]{2,1,0:T(8,128)} copy(f32[1,256,1024]{2,1,0:T(8,128)} %get-tuple-element.6) | data formatting | bytes 2097152
  87.7 0.0 copy-done.1
  87.7 0.0 copy-start
  87.7 1.0 %copy.12 = f32[1,256,1024]{2,1,0:T(8,128)} copy(f32[1,256,1024]{2,1,0:T(8,128)S(1)} %copy-done.1) | data formatting | bytes 2097152
  88.7 0.6 copy-done
  89.3 1.0 %copy.13 = f32[1,256,1024]{2,1,0:T(8,128)} copy(f32[1,256,1024]{2,1,0:T(8,128)S(1)} %copy-done) | data formatting | bytes 2097152
Async XLA Ops:
  85.3 2.4 %copy-start.1 = (f32[1,256,1024]{2,1,0:T(8,128)S(1)}, f32[1,256,1024]{2,1,0:T(8,128)}, u32[]{:S(2)}) copy-start(f32[1,256,1024]{2,1,0:T(8,128)} %get-tuple-element.7) | copy-start | bytes 3145732
  87.7 1.6 %copy-start = (f32[1,256,1024]{2,1,0:T(8,128)S(1)}, f32[1,256,1024]{2,1,0:T(8,128)}, u32[]{:S(2)}) copy-start(f32[1,256,1024]{2,1,0:T(8,128)} %get-tuple-element.8) | copy-start | bytes 3145732

commit v2 on v1

--- a/solution.py
+++ b/solution.py
@@ -115,7 +115,7 @@
                 pack[side, f, pl.ds(pl.multiple_of(g * SUB, SUB), SUB), :] = packed
             return carry
 
-        lax.fori_loop(0, rows // 32, pack_group, 0)
+        lax.fori_loop(0, rows // 32, pack_group, 0, unroll=4)
     deep = rows // 4
     col_copies = []
     for side, device in ((0, right), (1, left)):
@@ -143,13 +143,73 @@
     for c in range(1, tiles - 1):
         for f in range(3):
             loads[f, c].wait()
-    for copy in row_copies:
-        copy.wait()
-    for f in range(3):
-        for c in range(tiles):
-            cols = pl.ds(c * LANES, LANES)
-            fields[f, c, pl.ds(0, HALO), :] = row_halo[0, f, :, cols]
-            fields[f, c, pl.ds(HALO + rows, HALO), :] = row_halo[1, f, :, cols]
+    def lane_pairs(values, distance):
+        to_right = [pltpu.roll(v, distance, 1) for v in values]
+        to_left = [pltpu.roll(v, LANES - distance, 1) for v in values]
+        from_left = [
+            jnp.where(lane < distance, to_right[c - 1], to_right[c]) for c in range(len(values))
+        ]
+        from_right = [
+            jnp.where(lane >= LANES - distance, to_left[(c + 1) % len(values)], to_left[c])
+            for c in range(len(values))
+        ]
+        return from_left, from_right
+
+    factor = explicit_weight * advect_courant
+    half_wave = 0.5 * wave
+
+    def section(first, last, chosen, unroll):
+        def body(i, carry):
+            base = pl.multiple_of(i * SUB, SUB)
+            at, up, down = (pl.ds(base + k, SUB) for k in (7, 6, 8))
+            mids, to_right, to_left = {}, {}, {}
+
+            def mid_of(f, c):
+                if (f, c) not in mids:
+                    mids[f, c] = fields[f, c, at, :]
+                return mids[f, c]
+
+            def shifted(f, c):
+                before, after = (c - 1) % ring, (c + 1) % ring
+                for k in (before, c):
+                    if (f, k) not in to_right:
+                        to_right[f, k] = pltpu.roll(mid_of(f, k), 1, 1)
+                for k in (c, after):
+                    if (f, k) not in to_left:
+                        to_left[f, k] = pltpu.roll(mid_of(f, k), LANES - 1, 1)
+                west = jnp.where(lane < 1, to_right[f, before], to_right[f, c])
+                return west, jnp.where(lane >= LANES - 1, to_left[f, after], to_left[f, c])
+
+            for c in chosen:
+                u, v = mid_of(1, c), mid_of(2, c)
+                east = u > 0
+                north = v > 0
+                fu = factor * u
+                fv = factor * v
+                moved = []
+                grads = []
+                for f in range(3):
+                    w, e = shifted(f, c)
+                    s, n = fields[f, c, up, :], fields[f, c, down, :]
+                    mid = mid_of(f, c)
+                    moved.append(
+                        mid
+                        - (
+                            fu * jnp.where(east, mid - w, e - mid)
+                            + fv * jnp.where(north, mid - s, n - mid)
+                        )
+                    )
+                    grads.append((e - w, n - s))
+                src[c, at, :] = moved[0] - half_wave * (grads[1][0] + grads[2][1])
+                su[c, at, :] = moved[1] - half_wave * grads[0][0]
+                sv[c, at, :] = moved[2] - half_wave * grads[0][1]
+            return carry
+
+        lax.fori_loop(first, last, body, 0, unroll=unroll)
+
+    begin = HALO // SUB
+    end = begin + rows // SUB - 1
+    section(begin, end, range(1, tiles - 1), 4)
     for copy in col_copies:
         copy.wait()
     for f in range(3):
@@ -166,55 +226,18 @@
                 fields[f, tiles, pl.ds(start, SUB), :] = jnp.where(lane < 64, a, b)
             return carry
 
-        lax.fori_loop(0, (rows + 2 * HALO) // 32, unpack_group, 0)
-
-    def lane_pairs(values, distance):
-        to_right = [pltpu.roll(v, distance, 1) for v in values]
-        to_left = [pltpu.roll(v, LANES - distance, 1) for v in values]
-        from_left = [
-            jnp.where(lane < distance, to_right[c - 1], to_right[c]) for c in range(len(values))
-        ]
-        from_right = [
-            jnp.where(lane >= LANES - distance, to_left[(c + 1) % len(values)], to_left[c])
-            for c in range(len(values))
-        ]
-        return from_left, from_right
-
-    factor = explicit_weight * advect_courant
-    half_wave = 0.5 * wave
-
-    def section(i, carry):
-        base = pl.multiple_of(i * SUB, SUB)
-        at, up, down = (pl.ds(base + k, SUB) for k in (7, 6, 8))
-        h = [fields[0, c, at, :] for c in range(ring)]
-        u = [fields[1, c, at, :] for c in range(ring)]
-        v = [fields[2, c, at, :] for c in range(ring)]
-        sides = [lane_pairs(q, 1) for q in (h, u, v)]
-        for c in range(ring):
-            east = u[c] > 0
-            north = v[c] > 0
-            fu = factor * u[c]
-            fv = factor * v[c]
-            moved = []
-            grads = []
-            for f, q in enumerate((h, u, v)):
-                w, e = sides[f][0][c], sides[f][1][c]
-                s, n = fields[f, c, up, :], fields[f, c, down, :]
-                mid = q[c]
-                moved.append(
-                    mid
-                    - (
-                        fu * jnp.where(east, mid - w, e - mid)
-                        + fv * jnp.where(north, mid - s, n - mid)
-                    )
-                )
-                grads.append((e - w, n - s))
-            src[c, at, :] = moved[0] - half_wave * (grads[1][0] + grads[2][1])
-            su[c, at, :] = moved[1] - half_wave * grads[0][0]
-            sv[c, at, :] = moved[2] - half_wave * grads[0][1]
-        return carry
-
-    lax.fori_loop(0, (rows + 2 * HALO) // SUB - 1, section, 0)
+        lax.fori_loop(0, (rows + 2 * HALO) // 32, unpack_group, 0, unroll=5)
+
+    section(begin, end, (tiles - 1, tiles, 0), 4)
+    for copy in row_copies:
+        copy.wait()
+    for f in range(3):
+        for c in range(tiles):
+            cols = pl.ds(c * LANES, LANES)
+            fields[f, c, pl.ds(0, HALO), :] = row_halo[0, f, :, cols]
+            fields[f, c, pl.ds(HALO + rows, HALO), :] = row_halo[1, f, :, cols]
+    section(0, begin, range(ring), 4)
+    section(end, end + begin, range(ring), 4)
 
     def source(i, carry):
         base = pl.multiple_of(i * SUB, SUB)
@@ -225,7 +248,7 @@
             src[c, at, :] = src[c, at, :] - half_wave * grad
         return carry
 
-    lax.fori_loop(1, (rows + 2 * HALO) // SUB - 1, source, 0)
+    lax.fori_loop(1, (rows + 2 * HALO) // SUB - 1, source, 0, unroll=8)
 
     def neighbour_sums(ref, base):
         mids = [ref[c, pl.ds(base, SUB), :] for c in range(ring)]
@@ -248,7 +271,7 @@
                 out[c, pl.ds(base, SUB), :] = combine(c, base, mids[c], sums[c])
             return carry
 
-        lax.fori_loop(lo, hi, body, 0)
+        lax.fori_loop(lo, hi, body, 0, unroll=8)
 
     def precondition_half(step, r, z, first):
         at = lambda c, base: r[c, pl.ds(base, SUB), :]
@@ -273,7 +296,7 @@
 
         zero = jnp.zeros((SUB, LANES), jnp.float32)
         first, second = lax.fori_loop(
-            0, rows // SUB, body, ([zero, zero], [zero, zero])
+            0, rows // SUB, body, ([zero, zero], [zero, zero]), unroll=8
         )
         red_send[index, 0, pl.ds(0, 1), :] = jnp.sum(first[0] + first[1], axis=0, keepdims=True)
         red_send[index, 0, pl.ds(1, 1), :] = jnp.sum(second[0] + second[1], axis=0, keepdims=True)
@@ -379,7 +402,7 @@
             solved[c, at, :] = take_z0 * z0[c, at, :] + take_m0 * m0[c, at, :] + take_m1 * m1[c, at, :]
         return carry
 
-    lax.fori_loop(HALO // SUB - 1, (HALO + rows) // SUB + 1, combine, 0)
+    lax.fori_loop(HALO // SUB - 1, (HALO + rows) // SUB + 1, combine, 0, unroll=4)
 
     outputs = (x_out, u_out, v_out)
     chunks = 4
@@ -401,7 +424,7 @@
                 stage[2, to, cols] = sv[c, at, :] - half_wave * (north - south)
             return carry
 
-        lax.fori_loop(0, chunk // SUB, finish, 0)
+        lax.fori_loop(0, chunk // SUB, finish, 0, unroll=4)
         for f in range(3):
             part = pl.ds(k * chunk, chunk)
             writes.append(

time: 90.5 us -> 59.8 us (0.66)
  Pallas kernels: 84 us -> 53.3 us
    pallas_call x1, Pallas kernels: 84 us -> 53.3 us  [local(): pl.pallas_call(functools.partial(kernel, nx, ny, rows, tiles), out_shape=...]
where the time goes in v2:
time: 59.8 us; the launch traced here: 59.6 us
  Pallas kernels  53.3 us (89%)
  local copies, waits for them, and re-layouts  4.97 us (8%)
  between operations  1.3 us (2%)
    pallas_call x1, Pallas kernels, local(): pl.pallas_call(functools.partial(kernel, nx, ny, rows, tiles), out_shape=...  53.3 us
    unnamed x7, local copies, waits for them, and re-layouts  4.97 us

profile of v2, /device:TPU:0, one launch (start us, length us, event | category | flops | bytes accessed | tf_op | source)
XLA Modules:
  0.0 59.6 jit_solution(15049616443112778385)
XLA Ops:
  1.3 53.3 %shard_map.67 = (f32[1,256,1024]{2,1,0:T(8,128)}, f32[1,256,1024]{2,1,0:T(8,128)}, f32[1,256,1024]{2,1,0:T(8,128)}) custom-call(f32[1]{0:T(128)S(6)} %copy.10.wave_ref, f32[1,256,1024]{2,1,0:T(8,128)} %h_in.1, f32[1,256,1024]{2,1,0:T(8,128)} %u_in.1, f32[1,256,1024]{2,1,0:T(8,128)} %v_in.1), custom_call_target="tpu_custom_call" | custom-call | tf_op jit(solution)/shard_map/pallas_call | solution.py:449
  54.6 0.0 copy-start.1
  54.6 2.4 %copy.11 = f32[1,256,1024]{2,1,0:T(8,128)} copy(f32[1,256,1024]{2,1,0:T(8,128)} %get-tuple-element.6) | data formatting | bytes 2097152
  57.0 0.0 copy-done.1
  57.0 0.0 copy-start
  57.0 1.0 %copy.12 = f32[1,256,1024]{2,1,0:T(8,128)} copy(f32[1,256,1024]{2,1,0:T(8,128)S(1)} %copy-done.1) | data formatting | bytes 2097152
  58.0 0.6 %copy-done = f32[1,256,1024]{2,1,0:T(8,128)S(1)} copy-done((f32[1,256,1024]{2,1,0:T(8,128)S(1)}, f32[1,256,1024]{2,1,0:T(8,128)}, u32[]{:S(2)}) %copy-start) | copy-done | bytes 1048600
  58.6 1.0 %copy.13 = f32[1,256,1024]{2,1,0:T(8,128)} copy(f32[1,256,1024]{2,1,0:T(8,128)S(1)} %copy-done) | data formatting | bytes 2097152
Async XLA Ops:
  54.6 2.4 %copy-start.1 = (f32[1,256,1024]{2,1,0:T(8,128)S(1)}, f32[1,256,1024]{2,1,0:T(8,128)}, u32[]{:S(2)}) copy-start(f32[1,256,1024]{2,1,0:T(8,128)} %get-tuple-element.7) | copy-start | bytes 3145732
  57.0 1.6 %copy-start = (f32[1,256,1024]{2,1,0:T(8,128)S(1)}, f32[1,256,1024]{2,1,0:T(8,128)}, u32[]{:S(2)}) copy-start(f32[1,256,1024]{2,1,0:T(8,128)} %get-tuple-element.8) | copy-start | bytes 3145732
